TPU v7x, 32 devices: a whole 2x2x4 slice. The times are simulated.
32 devices in a mesh: rep: 2 (over y), shard: 16 (over z, x, core).
Axes of the slice: x: 2, y: 2, z: 4, core: 2. Of those that a mesh axis runs over, the one named last changes fastest.
Arguments:
- images: bfloat16 [32, 14, 14, 512], P(('rep', 'shard')), may hold values from -6 to 6
- cotangent: bfloat16 [32, 14, 14, 512], P(('rep', 'shard')), may hold values from -6 to 6
- regions: int32 [32, 14, 14], P(('rep', 'shard')), may hold values from 0 to 8, as said below
- w_qkv: bfloat16 [2, 512, 1536], P(None, 'shard'), may hold values from -0.25 to 0.25
- w_proj: bfloat16 [2, 512, 512], P(None, 'shard'), may hold values from -0.75 to 0.75
- w_fc1: bfloat16 [2, 512, 2048], P(None, 'shard'), may hold values from -0.25 to 0.25
- w_fc2: bfloat16 [2, 2048, 512], P(None, 'shard'), may hold values from -0.125 to 0.125
- norm_gains: bfloat16 [2, 2, 512], P(None, None, 'shard'), may hold values from 0.5 to 1.5
- norm_shifts: bfloat16 [2, 2, 512], P(None, None, 'shard'), may hold values from -1.1953125 to 1.1953125
- branch_biases: bfloat16 [2, 4, 512], P(None, None, 'shard'), may hold values from -1.1953125 to 1.1953125
- fc1_bias: bfloat16 [2, 2048], P(None, 'shard'), may hold values from -1.1953125 to 1.1953125
- rel_table: bfloat16 [2, 169, 16], replicated, may hold values from -6 to 6
Outputs:
- images_out: bfloat16 [32, 14, 14, 512], P(('rep', 'shard'))
- images_grad: float32 [32, 14, 14, 512], P(('rep', 'shard'))
- grad_w_qkv: float32 [2, 512, 1536], P(None, 'shard')
- grad_w_proj: float32 [2, 512, 512], P(None, 'shard')
- grad_w_fc1: float32 [2, 512, 2048], P(None, 'shard')
- grad_w_fc2: float32 [2, 2048, 512], P(None, 'shard')
- grad_norm_gains: float32 [2, 2, 512], P(None, None, 'shard')
- grad_norm_shifts: float32 [2, 2, 512], P(None, None, 'shard')
- grad_branch_biases: float32 [2, 4, 512], P(None, None, 'shard')
- grad_fc1_bias: float32 [2, 2048], P(None, 'shard')
- grad_rel_table: float32 [2, 169, 16], replicated
Inputs may be any that keep to these rules, and one draw needn't show every extreme that they name: `regions`: in each image the ids are 3 * (row band) + (column band), the rows and the columns each cut into three bands of consecutive positions.
All inputs are finite; a program needn't handle non-finite values.
Results may differ from a plain program's by a relative error of at most 0.023.
Values may be sent and summed in bfloat16 or wider, within the bound.
A program may use at most 128 MiB of HBM per device.

v0:
```python
import jax
import jax.numpy as jnp
from jax import lax
from jax.sharding import PartitionSpec as P

SIDE = 14
WIN = 7
SHIFT = 3
eps = 1e-05
highest = lax.Precision.HIGHEST
inv_root_two = 0.7071067811865476
inv_root_two_pi = 0.3989422804014327


def layer_norm(values, norm_gain, norm_shift):
    row_mean = jnp.mean(values, axis=-1, keepdims=True)
    centred = values - row_mean
    row_var = jnp.mean(centred * centred, axis=-1, keepdims=True)
    return centred * lax.rsqrt(row_var + eps) * norm_gain + norm_shift


def times_transposed(left, right):
    return lax.dot_general(
        left, right, (((1,), (1,)), ((), ())), preferred_element_type=jnp.float32
    )


def transposed_times(left, right):
    return lax.dot_general(
        left, right, (((0,), (0,)), ((), ())), preferred_element_type=jnp.float32
    )


def gelu_slope(pre_act):
    return 0.5 * (1.0 + lax.erf(pre_act * inv_root_two)) + pre_act * inv_root_two_pi * jnp.exp(
        -0.5 * pre_act * pre_act
    )


def to_windows(grid_data):
    image_count = grid_data.shape[0]
    per_side = SIDE // WIN
    trailing = grid_data.shape[3:]
    blocks = grid_data.reshape((image_count, per_side, WIN, per_side, WIN) + trailing)
    blocks = jnp.swapaxes(blocks, 2, 3)
    return blocks.reshape((image_count * per_side * per_side, WIN * WIN) + trailing)


def from_windows(blocks, image_count):
    per_side = SIDE // WIN
    trailing = blocks.shape[2:]
    grid_data = blocks.reshape((image_count, per_side, per_side, WIN, WIN) + trailing)
    grid_data = jnp.swapaxes(grid_data, 2, 3)
    return grid_data.reshape((image_count, SIDE, SIDE) + trailing)


def onehot_table():
    cell_ids = jnp.arange(WIN * WIN)
    cell_row = cell_ids // WIN
    cell_col = cell_ids % WIN
    table_side = 2 * WIN - 1
    rel_index = (cell_row[:, None] - cell_row[None, :] + WIN - 1) * table_side + (
        cell_col[:, None] - cell_col[None, :] + WIN - 1
    )
    rel_index = rel_index.reshape(-1)
    return (rel_index[:, None] == jnp.arange(table_side * table_side)[None, :]).astype(jnp.float32)


def replica_total(stacked):
    return (
        lax.psum(stacked[0].astype(jnp.bfloat16), "rep").astype(jnp.float32),
        lax.psum(stacked[1].astype(jnp.bfloat16), "rep").astype(jnp.float32),
        lax.psum(stacked[2].astype(jnp.bfloat16), "rep").astype(jnp.float32),
        lax.psum(stacked[3].astype(jnp.bfloat16), "rep").astype(jnp.float32),
        lax.psum(stacked[4].astype(jnp.bfloat16), "rep").astype(jnp.float32),
        lax.psum(stacked[5].astype(jnp.bfloat16), "rep").astype(jnp.float32),
        lax.psum(stacked[6].astype(jnp.bfloat16), "rep").astype(jnp.float32),
        lax.psum(stacked[7].astype(jnp.bfloat16), "rep").astype(jnp.float32),
    )


def body(
    images,
    cotangent,
    regions,
    w_qkv,
    w_proj,
    w_fc1,
    w_fc2,
    norm_gains,
    norm_shifts,
    branch_biases,
    fc1_bias,
    rel_table,
):
    layer_count = w_qkv.shape[0]
    image_count = images.shape[0]
    model_width = w_proj.shape[2]
    head_count = rel_table.shape[2]
    head_dim = model_width // head_count
    query_scale = head_dim ** (-0.5)
    column_scale = jnp.concatenate(
        [
            jnp.full((model_width,), query_scale, jnp.float32),
            jnp.ones((2 * model_width,), jnp.float32),
        ]
    )
    onehot = onehot_table()
    region_win = to_windows(regions)
    region_mask = jnp.where(region_win[:, :, None] == region_win[:, None, :], 0.0, -100.0).astype(
        jnp.float32
    )
    window_count = region_win.shape[0]
    tokens = window_count * WIN * WIN

    def score_bias(layer_num):
        table_rows = jnp.dot(onehot, rel_table[layer_num].astype(jnp.float32), precision=highest)
        bias_full = table_rows.T.reshape(head_count, WIN * WIN, WIN * WIN)[None]
        if layer_num % 2 == 1:
            bias_full = bias_full + region_mask[:, None]
        return bias_full

    def heads_of(flat):
        return flat.reshape(window_count, WIN * WIN, head_count, head_dim)

    residual = images.astype(jnp.float32)
    saved_acts = []
    kept_weights = []
    for layer_num in range(layer_count):
        shifted = layer_num % 2 == 1
        attn_w = (
            lax.all_gather(w_qkv[layer_num], "shard", axis=0, tiled=True),
            lax.all_gather(w_proj[layer_num], "shard", axis=0, tiled=True),
            lax.all_gather(norm_gains[layer_num], "shard", axis=1, tiled=True),
            lax.all_gather(norm_shifts[layer_num], "shard", axis=1, tiled=True),
            lax.all_gather(branch_biases[layer_num], "shard", axis=1, tiled=True),
        )
        mlp_w = (
            lax.all_gather(w_fc1[layer_num], "shard", axis=0, tiled=True),
            lax.all_gather(w_fc2[layer_num], "shard", axis=0, tiled=True),
            lax.all_gather(fc1_bias[layer_num], "shard", axis=0, tiled=True),
        )
        kept_weights.append((attn_w, mlp_w))
        wqkv, wproj, gains, shifts, biases = attn_w
        gains = gains.astype(jnp.float32)
        shifts = shifts.astype(jnp.float32)
        biases = biases.astype(jnp.float32)
        normed = layer_norm(residual, gains[0], shifts[0]).astype(jnp.bfloat16)
        if shifted:
            normed = jnp.roll(normed, (-SHIFT, -SHIFT), axis=(1, 2))
        window_rows = to_windows(normed).reshape(tokens, model_width)
        projected = jnp.dot(window_rows, wqkv, preferred_element_type=jnp.float32)
        queries = heads_of(
            ((projected[:, :model_width] + biases[0]) * query_scale).astype(jnp.bfloat16)
        )
        key_rows = heads_of(projected[:, model_width : 2 * model_width].astype(jnp.bfloat16))
        values = heads_of((projected[:, 2 * model_width :] + biases[1]).astype(jnp.bfloat16))
        scores = jnp.einsum(
            "nqhd,nkhd->nhqk", queries, key_rows, preferred_element_type=jnp.float32
        ) + score_bias(layer_num)
        row_max = jnp.max(scores, axis=-1, keepdims=True)
        log_total = row_max + jnp.log(jnp.sum(jnp.exp(scores - row_max), axis=-1, keepdims=True))
        attn_probs = jnp.exp(scores - log_total).astype(jnp.bfloat16)
        mixed_rows = jnp.einsum(
            "nhqk,nkhd->nqhd", attn_probs, values, preferred_element_type=jnp.float32
        )
        mixed_rows = mixed_rows.reshape(tokens, model_width).astype(jnp.bfloat16)
        branch = jnp.dot(mixed_rows, wproj, preferred_element_type=jnp.float32) + biases[2]
        branch = from_windows(branch.reshape(window_count, WIN * WIN, model_width), image_count)
        if shifted:
            branch = jnp.roll(branch, (SHIFT, SHIFT), axis=(1, 2))
        middle = residual + branch
        wfirst, wsecond, bias_first = mlp_w
        normed_mlp = (
            layer_norm(middle, gains[1], shifts[1]).astype(jnp.bfloat16).reshape(-1, model_width)
        )
        pre_act = jnp.dot(
            normed_mlp, wfirst, preferred_element_type=jnp.float32
        ) + bias_first.astype(jnp.float32)
        activated = jax.nn.gelu(pre_act, approximate=False).astype(jnp.bfloat16)
        mlp_out = jnp.dot(activated, wsecond, preferred_element_type=jnp.float32) + biases[3]
        saved_acts.append(
            (
                residual,
                window_rows,
                queries,
                key_rows,
                values,
                log_total,
                mixed_rows,
                middle,
                normed_mlp,
                pre_act,
                activated,
            )
        )
        residual = middle + mlp_out.reshape(middle.shape)
    images_out = residual.astype(jnp.bfloat16)
    upstream = cotangent.astype(jnp.float32)
    layer_grads = [None] * layer_count
    table_list = [None] * layer_count
    for layer_num in reversed(range(layer_count)):
        shifted = layer_num % 2 == 1
        (
            residual_in,
            window_rows,
            queries,
            key_rows,
            values,
            log_total,
            mixed_rows,
            middle,
            normed_mlp,
            pre_act,
            activated,
        ) = saved_acts[layer_num]
        wqkv, wproj, gains, shifts, biases = (
            lax.all_gather(w_qkv[layer_num], "shard", axis=0, tiled=True),
            lax.all_gather(w_proj[layer_num], "shard", axis=0, tiled=True),
            lax.all_gather(norm_gains[layer_num], "shard", axis=1, tiled=True),
            lax.all_gather(norm_shifts[layer_num], "shard", axis=1, tiled=True),
            lax.all_gather(branch_biases[layer_num], "shard", axis=1, tiled=True),
        )
        wfirst, wsecond, bias_first = (
            lax.all_gather(w_fc1[layer_num], "shard", axis=0, tiled=True),
            lax.all_gather(w_fc2[layer_num], "shard", axis=0, tiled=True),
            lax.all_gather(fc1_bias[layer_num], "shard", axis=0, tiled=True),
        )
        gains = gains.astype(jnp.float32)
        shifts = shifts.astype(jnp.float32)
        out_grad = upstream.astype(jnp.bfloat16).reshape(-1, model_width)
        grad_b_second = jnp.sum(out_grad.astype(jnp.float32), axis=0)
        grad_w_second = transposed_times(activated, out_grad)
        act_grad = times_transposed(out_grad, wsecond)
        pre_grad = (act_grad * gelu_slope(pre_act)).astype(jnp.bfloat16)
        grad_b_first = jnp.sum(pre_grad.astype(jnp.float32), axis=0)
        grad_w_first = transposed_times(normed_mlp, pre_grad)
        norm_grad = times_transposed(pre_grad, wfirst).reshape(middle.shape)
        norm_pull = jax.vjp(layer_norm, middle, gains[1], shifts[1])[1]
        middle_part, grad_gain_mlp, grad_shift_mlp = norm_pull(norm_grad)
        middle_grad = upstream + middle_part
        branch_grad = middle_grad
        if shifted:
            branch_grad = jnp.roll(branch_grad, (-SHIFT, -SHIFT), axis=(1, 2))
        branch_rows = to_windows(branch_grad.astype(jnp.bfloat16)).reshape(tokens, model_width)
        grad_b_proj = jnp.sum(branch_rows.astype(jnp.float32), axis=0)
        grad_w_proj = transposed_times(mixed_rows, branch_rows)
        mixed_grad = heads_of(times_transposed(branch_rows, wproj).astype(jnp.bfloat16))
        scores = jnp.einsum(
            "nqhd,nkhd->nhqk", queries, key_rows, preferred_element_type=jnp.float32
        ) + score_bias(layer_num)
        attn_probs = jnp.exp(scores - log_total)
        prob_grad = jnp.einsum(
            "nqhd,nkhd->nhqk", mixed_grad, values, preferred_element_type=jnp.float32
        )
        value_grad = jnp.einsum(
            "nhqk,nqhd->nkhd",
            attn_probs.astype(jnp.bfloat16),
            mixed_grad,
            preferred_element_type=jnp.float32,
        ).astype(jnp.bfloat16)
        score_grad = (
            attn_probs * (prob_grad - jnp.sum(attn_probs * prob_grad, axis=-1, keepdims=True))
        ).astype(jnp.bfloat16)
        table_term = jnp.sum(score_grad.astype(jnp.float32), axis=0).reshape(head_count, -1).T
        table_list[layer_num] = jnp.dot(onehot.T, table_term, precision=highest)
        query_grad = jnp.einsum(
            "nhqk,nkhd->nqhd", score_grad, key_rows, preferred_element_type=jnp.float32
        ).astype(jnp.bfloat16)
        key_grad = jnp.einsum(
            "nhqk,nqhd->nkhd", score_grad, queries, preferred_element_type=jnp.float32
        ).astype(jnp.bfloat16)
        qkv_grad = jnp.concatenate(
            [
                query_grad.reshape(tokens, model_width),
                key_grad.reshape(tokens, model_width),
                value_grad.reshape(tokens, model_width),
            ],
            axis=1,
        )
        grad_w_proj_qkv = transposed_times(window_rows, qkv_grad) * column_scale[None, :]
        grad_b_query = (
            jnp.sum(query_grad.reshape(tokens, model_width).astype(jnp.float32), axis=0)
            * query_scale
        )
        grad_b_value = jnp.sum(value_grad.reshape(tokens, model_width).astype(jnp.float32), axis=0)
        rows_grad = times_transposed(qkv_grad[:, :model_width], wqkv[:, :model_width]) * query_scale
        rows_grad = rows_grad + times_transposed(qkv_grad[:, model_width:], wqkv[:, model_width:])
        normed_grad = from_windows(
            rows_grad.reshape(window_count, WIN * WIN, model_width), image_count
        )
        if shifted:
            normed_grad = jnp.roll(normed_grad, (SHIFT, SHIFT), axis=(1, 2))
        first_pull = jax.vjp(layer_norm, residual_in, gains[0], shifts[0])[1]
        input_part, grad_gain_attn, grad_shift_attn = first_pull(normed_grad)
        upstream = middle_grad + input_part
        gain_grads = jnp.stack([grad_gain_attn, grad_gain_mlp])
        shift_grads = jnp.stack([grad_shift_attn, grad_shift_mlp])
        bias_grads = jnp.stack([grad_b_query, grad_b_value, grad_b_proj, grad_b_second])
        qkv_share, proj_share, gain_share, shift_share, bias_share = (
            lax.psum_scatter(
                grad_w_proj_qkv.astype(jnp.bfloat16), "shard", scatter_dimension=0, tiled=True
            ).astype(jnp.float32),
            lax.psum_scatter(
                grad_w_proj.astype(jnp.bfloat16), "shard", scatter_dimension=0, tiled=True
            ).astype(jnp.float32),
            lax.psum_scatter(
                gain_grads.astype(jnp.bfloat16), "shard", scatter_dimension=1, tiled=True
            ).astype(jnp.float32),
            lax.psum_scatter(
                shift_grads.astype(jnp.bfloat16), "shard", scatter_dimension=1, tiled=True
            ).astype(jnp.float32),
            lax.psum_scatter(
                bias_grads.astype(jnp.bfloat16), "shard", scatter_dimension=1, tiled=True
            ).astype(jnp.float32),
        )
        first_share, second_share, bfirst_share = (
            lax.psum_scatter(
                grad_w_first.astype(jnp.bfloat16), "shard", scatter_dimension=0, tiled=True
            ).astype(jnp.float32),
            lax.psum_scatter(
                grad_w_second.astype(jnp.bfloat16), "shard", scatter_dimension=0, tiled=True
            ).astype(jnp.float32),
            lax.psum_scatter(
                grad_b_first.astype(jnp.bfloat16), "shard", scatter_dimension=0, tiled=True
            ).astype(jnp.float32),
        )
        layer_grads[layer_num] = (
            qkv_share,
            proj_share,
            first_share,
            second_share,
            gain_share,
            shift_share,
            bias_share,
            bfirst_share,
        )
    stacked = [jnp.stack([layer_grads[n][m] for n in range(layer_count)]) for m in range(8)]
    summed = replica_total(stacked)
    table_total = lax.psum(jnp.stack(table_list), ("rep", "shard"))
    return (
        images_out,
        upstream,
        summed[0],
        summed[1],
        summed[2],
        summed[3],
        summed[4],
        summed[5],
        summed[6],
        summed[7],
        table_total,
    )


def solution(mesh):
    return jax.shard_map(
        body,
        mesh=mesh,
        in_specs=(
            P(("rep", "shard"), None, None, None),
            P(("rep", "shard"), None, None, None),
            P(("rep", "shard"), None, None),
            P(None, "shard", None),
            P(None, "shard", None),
            P(None, "shard", None),
            P(None, "shard", None),
            P(None, None, "shard"),
            P(None, None, "shard"),
            P(None, None, "shard"),
            P(None, "shard"),
            P(),
        ),
        out_specs=(
            P(("rep", "shard"), None, None, None),
            P(("rep", "shard"), None, None, None),
            P(None, "shard", None),
            P(None, "shard", None),
            P(None, "shard", None),
            P(None, "shard", None),
            P(None, None, "shard"),
            P(None, None, "shard"),
            P(None, None, "shard"),
            P(None, "shard"),
            P(),
        ),
        check_vma=False,
    )
```

profile of v0, /device:TPU:0, one launch (start us, length us, event | category | flops | bytes accessed | tf_op | source)
XLA Modules:
  0.0 1341.8 jit_solution(16533433941194631323)
XLA Ops:
  17.5 24.0 %all-gather = bf16[1,2,512]{1,0,2:T(2,128)(2,1)S(1)} all-gather(bf16[1,2,32]{1,0,2:T(2,128)(2,1)S(1)} %copy.412), channel_id=2, replica_groups=mesh['rep'=2,'shard'=16] {'shard'}, dimensions={2}, use_global_device_ids=true | all-gather | bytes 2176 | tf_op jit(solution)/shard_map/all_gather | solution.py:134
  41.7 2.7 slice_reduce_fusion.10
  44.6 18.3 %all-gather.1 = bf16[1,2,512]{1,0,2:T(2,128)(2,1)S(1)} all-gather(bf16[1,2,32]{1,0,2:T(2,128)(2,1)S(1)} %copy.413), channel_id=3, replica_groups=mesh['rep'=2,'shard'=16] {'shard'}, dimensions={2}, use_global_device_ids=true | all-gather | bytes 2176 | tf_op jit(solution)/shard_map/all_gather | solution.py:135
  63.1 2.7 slice_reduce_fusion.9
  67.9 20.7 %all-gather.3 = bf16[1,4,512]{1,0,2:T(2,128)(2,1)S(1)} all-gather(bf16[1,4,32]{1,0,2:T(2,128)(2,1)S(1)} %copy.414), channel_id=5, replica_groups=mesh['rep'=2,'shard'=16] {'shard'}, dimensions={2}, use_global_device_ids=true | all-gather | bytes 4352 | tf_op jit(solution)/shard_map/all_gather | solution.py:136
  88.9 6.7 slice_reduce_fusion.8
  96.1 19.4 %all-gather.4 = bf16[1,512,512]{2,1,0:T(8,128)(2,1)S(1)} all-gather(bf16[1,32,512]{2,1,0:T(8,128)(2,1)S(1)} %get-tuple-element.155), channel_id=6, replica_groups=mesh['rep'=2,'shard'=16] {'shard'}, dimensions={1}, use_global_device_ids=true | all-gather | bytes 557056 | tf_op jit(solution)/shard_map/all_gather | solution.py:133
  115.5 18.6 %all-gather.6 = bf16[1,2048]{1,0:T(2,128)(2,1)S(1)} all-gather(bf16[1,128]{1,0:T(2,128)(2,1)S(1)} %get-tuple-element.163), channel_id=8, replica_groups=mesh['rep'=2,'shard'=16] {'shard'}, dimensions={1}, use_global_device_ids=true | all-gather | bytes 4352 | tf_op jit(solution)/shard_map/all_gather | solution.py:141
  134.3 18.2 %all-gather.8 = bf16[1,2,512]{1,0,2:T(2,128)(2,1)S(1)} all-gather(bf16[1,2,32]{1,0,2:T(2,128)(2,1)S(1)} %copy.415), channel_id=10, replica_groups=mesh['rep'=2,'shard'=16] {'shard'}, dimensions={2}, use_global_device_ids=true | all-gather | bytes 2176 | tf_op jit(solution)/shard_map/all_gather | solution.py:134
  152.7 3.3 slice_reduce_fusion.2
  156.2 19.6 %all-gather.9 = bf16[1,2,512]{1,0,2:T(2,128)(2,1)S(1)} all-gather(bf16[1,2,32]{1,0,2:T(2,128)(2,1)S(1)} %copy.416), channel_id=11, replica_groups=mesh['rep'=2,'shard'=16] {'shard'}, dimensions={2}, use_global_device_ids=true | all-gather | bytes 2176 | tf_op jit(solution)/shard_map/all_gather | solution.py:135
  176.0 3.3 slice_reduce_fusion.1
  179.4 31.4 %all-gather.11 = bf16[1,4,512]{1,0,2:T(2,128)(2,1)S(1)} all-gather(bf16[1,4,32]{1,0,2:T(2,128)(2,1)S(1)} %copy.417), channel_id=13, replica_groups=mesh['rep'=2,'shard'=16] {'shard'}, dimensions={2}, use_global_device_ids=true | all-gather | bytes 4352 | tf_op jit(solution)/shard_map/all_gather | solution.py:136
  211.1 7.3 slice_reduce_fusion
  220.6 21.8 %all-gather.12 = bf16[1,512,512]{2,1,0:T(8,128)(2,1)} all-gather(bf16[1,32,512]{2,1,0:T(8,128)(2,1)S(1)} %get-tuple-element.154), channel_id=14, replica_groups=mesh['rep'=2,'shard'=16] {'shard'}, dimensions={1}, use_global_device_ids=true | all-gather | bytes 557056 | tf_op jit(solution)/shard_map/all_gather | solution.py:133
  242.4 17.3 %all-gather.14 = bf16[1,2048]{1,0:T(2,128)(2,1)S(1)} all-gather(bf16[1,128]{1,0:T(2,128)(2,1)S(1)} %get-tuple-element.162), channel_id=16, replica_groups=mesh['rep'=2,'shard'=16] {'shard'}, dimensions={1}, use_global_device_ids=true | all-gather | bytes 4352 | tf_op jit(solution)/shard_map/all_gather | solution.py:141
  271.0 2.6 copy.312
  283.9 7.4 fusion.20
  291.3 3.2 fusion.57
  305.0 2.6 copy.324
  309.0 2.6 copy.325
  311.6 2.3 reshape.792
  313.9 2.6 copy.328
  334.2 7.0 fusion.23
  341.3 3.9 fusion.150
  347.4 2.2 reshape.795
  349.6 4.6 multiply_reduce_fusion.2
  354.8 3.2 fusion.60
  358.0 2.3 reshape.774
  360.3 5.4 fusion.130
  377.5 2.3 reshape.796
  379.9 2.6 copy.337
  382.5 2.7 multiply_reduce_fusion.1
  394.1 2.2 copy.347
  398.5 2.2 copy.341
  404.3 2.7 convolution_add_fusion.3
  414.6 4.8 multiply_reduce_fusion.3
  419.4 4.3 fusion.129
  423.8 2.7 convert_reduce_fusion.6
  426.5 3.9 fusion.151
  432.3 3.7 multiply_reduce_fusion.4
  436.1 3.4 fusion.128
  439.5 2.7 convert_reduce_fusion.4
  443.4 2.3 reshape.798
  447.5 3.4 multiply_reduce_fusion
  451.2 3.0 convert_reduce_fusion.1
  490.2 3.1 multiply_reduce_fusion.5
  493.4 3.4 fusion.127
  497.7 31.7 %all-reduce.2 = (bf16[2048]{0:T(1024)(128)(2,1)S(1)}, bf16[2048]{0:T(1024)(128)(2,1)S(1)}) all-reduce(bf16[2048]{0:T(1024)(128)(2,1)S(1)} %copy-done.107, bf16[2048]{0:T(1024)(128)(2,1)S(1)} %copy-done.108), channel_id=33, replica_groups=mesh['rep'=2,'shard'=16] {'shard'}, use_global_device_ids=true, to_apply=%region_63.64.clone | all-reduce | flops 4096 | bytes 16384
  534.4 37.7 %psum.71 = f32[2,169,16]{1,2,0:T(8,128)} all-reduce(f32[2,169,16]{1,2,0:T(8,128)S(1)} %pad_maximum_fusion.10), channel_id=1, replica_groups=mesh['rep'=2,'shard'=16] {'rep','shard'}, use_global_device_ids=true, to_apply=%region_67.68 | all-reduce | flops 5408 | bytes 43264 | tf_op jit(solution)/shard_map/psum | solution.py:340
  573.6 53.1 %reduce-scatter.27.cloned.1.call-done = bf16[32,1536]{1,0:T(8,128)(2,1)} async-done(((bf16[512,1536]{1,0:T(8,128)(2,1)}), bf16[32,1536]{1,0:T(8,128)(2,1)}) %reduce-scatter.27.cloned.1.call-update) | async-done | bytes 98320 | tf_op jit(solution)/shard_map/reduce_scatter | solution.py:301
  626.7 62.5 %reduce-scatter.29.cloned.1.call-done = bf16[32,1536]{1,0:T(8,128)(2,1)} async-done(((bf16[512,1536]{1,0:T(8,128)(2,1)}), bf16[32,1536]{1,0:T(8,128)(2,1)}) %reduce-scatter.29.cloned.1.call-update) | async-done | bytes 98320 | tf_op jit(solution)/shard_map/reduce_scatter | solution.py:301
  690.8 62.7 %reduce-scatter.37.cloned.1.call-done = bf16[32,2048]{1,0:T(8,128)(2,1)} async-done(((bf16[512,2048]{1,0:T(8,128)(2,1)}), bf16[32,2048]{1,0:T(8,128)(2,1)}) %reduce-scatter.37.cloned.1.call-update) | async-done | bytes 131088 | tf_op jit(solution)/shard_map/reduce_scatter | solution.py:318
  753.6 64.6 %reduce-scatter.35.cloned.1.call-done = bf16[32,2048]{1,0:T(8,128)(2,1)} async-done(((bf16[512,2048]{1,0:T(8,128)(2,1)}), bf16[32,2048]{1,0:T(8,128)(2,1)}) %reduce-scatter.35.cloned.1.call-update) | async-done | bytes 131088 | tf_op jit(solution)/shard_map/reduce_scatter | solution.py:318
  819.9 62.6 %reduce-scatter.39.cloned.1.call-done = bf16[128,512]{1,0:T(8,128)(2,1)} async-done(((bf16[2048,512]{1,0:T(8,128)(2,1)}), bf16[128,512]{1,0:T(8,128)(2,1)}) %reduce-scatter.39.cloned.1.call-update) | async-done | bytes 131088 | tf_op jit(solution)/shard_map/reduce_scatter | solution.py:321
  882.4 64.7 %reduce-scatter.41.cloned.1.call-done = bf16[128,512]{1,0:T(8,128)(2,1)} async-done(((bf16[2048,512]{1,0:T(8,128)(2,1)}), bf16[128,512]{1,0:T(8,128)(2,1)}) %reduce-scatter.41.cloned.1.call-update) | async-done | bytes 131088 | tf_op jit(solution)/shard_map/reduce_scatter | solution.py:321
  950.1 54.4 %reduce-scatter.47.cloned.1.call-done = bf16[32,2]{1,0:T(8,128)(2,1)} async-done(((bf16[512,2]{1,0:T(8,128)(2,1)}), bf16[32,2]{1,0:T(8,128)(2,1)}) %reduce-scatter.47.cloned.1.call-update) | async-done | bytes 144
  1005.3 56.7 %reduce-scatter.49.cloned.1.call-done = bf16[32,2]{1,0:T(8,128)(2,1)} async-done(((bf16[512,2]{1,0:T(8,128)(2,1)}), bf16[32,2]{1,0:T(8,128)(2,1)}) %reduce-scatter.49.cloned.1.call-update) | async-done | bytes 144
  1062.8 56.7 %reduce-scatter.43.cloned.1.call-done = bf16[32,2]{1,0:T(8,128)(2,1)} async-done(((bf16[512,2]{1,0:T(8,128)(2,1)}), bf16[32,2]{1,0:T(8,128)(2,1)}) %reduce-scatter.43.cloned.1.call-update) | async-done | bytes 144
  1120.2 57.2 %reduce-scatter.45.cloned.1.call-done = bf16[32,2]{1,0:T(8,128)(2,1)} async-done(((bf16[512,2]{1,0:T(8,128)(2,1)}), bf16[32,2]{1,0:T(8,128)(2,1)}) %reduce-scatter.45.cloned.1.call-update) | async-done | bytes 144
  1178.3 56.8 %reduce-scatter.51.cloned.1.call-done = bf16[32,4]{1,0:T(8,128)(2,1)} async-done(((bf16[512,4]{1,0:T(8,128)(2,1)}), bf16[32,4]{1,0:T(8,128)(2,1)}) %reduce-scatter.51.cloned.1.call-update) | async-done | bytes 272
  1235.8 56.7 %reduce-scatter.53.cloned.1.call-done = bf16[32,4]{1,0:T(8,128)(2,1)} async-done(((bf16[512,4]{1,0:T(8,128)(2,1)}), bf16[32,4]{1,0:T(8,128)(2,1)}) %reduce-scatter.53.cloned.1.call-update) | async-done | bytes 272
  1293.3 5.0 all-reduce.3
  1300.6 28.8 %all-reduce.7.cloned.1.call-done = (bf16[2,32,1536]{2,1,0:T(8,128)(2,1)}, bf16[2,32,512]{2,1,0:T(8,128)(2,1)}, bf16[2,32,2048]{2,1,0:T(8,128)(2,1)}, bf16[2,128,512]{2,1,0:T(8,128)(2,1)}) async-done(((bf16[2,32,1536]{2,1,0:T(8,128)(2,1)}, bf16[2,32,512]{2,1,0:T(8,128)(2,1)}, bf16[2,32,2048]{2,1,0:T(8,128)(2,1)}, bf16[2,128,512]{2,1,0:T(8,128)(2,1)}), (bf16[2,32,1536]{2,1,0:T(8,128)(2,1)}, ...) | async-done | bytes 786448 | tf_op jit(solution)/shard_map/psum | solution.py:71
  (516 shorter events, 169.8 us)
Async XLA Ops:
  7.2 7.3 copy-start.113
  7.2 253.9 %all-gather.23.cloned.1.call-start = ((), (), s32[]{:S(2)}) async-start(), calls=%async_computation.22 | async-start | bytes 1671168 | tf_op jit(solution)/shard_map/all_gather | solution.py:132
  8.9 6.8 copy-start.2
  8.9 275.0 %all-gather.25.cloned.1.call-start = ((), (), s32[]{:S(2)}) async-start(), calls=%async_computation.23 | async-start | bytes 2228224 | tf_op jit(solution)/shard_map/all_gather | solution.py:139
  10.7 6.7 copy-start.111
  10.7 280.6 %all-gather.27.cloned.1.call-start = ((), (), s32[]{:S(2)}) async-start(), calls=%async_computation.24 | async-start | bytes 2228224 | tf_op jit(solution)/shard_map/all_gather | solution.py:140
  12.4 288.5 %all-gather.29.cloned.1.call-start = ((), (), s32[]{:S(2)}) async-start(), calls=%async_computation.25 | async-start | bytes 1671168 | tf_op jit(solution)/shard_map/all_gather | solution.py:132
  13.0 321.2 %all-gather.31.cloned.1.call-start = ((), (), s32[]{:S(2)}) async-start(), calls=%async_computation.26 | async-start | bytes 2228224 | tf_op jit(solution)/shard_map/all_gather | solution.py:139
  13.6 327.7 %all-gather.33.cloned.1.call-start = ((), (), s32[]{:S(2)}) async-start(), calls=%async_computation.27 | async-start | bytes 2228224 | tf_op jit(solution)/shard_map/all_gather | solution.py:140
  14.2 558.0 %reduce-scatter.33.cloned.1.call-start = ((), (), s32[]{:S(2)}) async-start(), calls=%async_computation.17 | async-start | bytes 557056 | tf_op jit(solution)/shard_map/reduce_scatter | solution.py:304
  14.3 30.1 %copy-start.112 = (bf16[2,2,32]{2,1,0:T(2,128)(2,1)S(1)}, bf16[2,2,32]{2,1,0:T(2,128)(2,1)}, u32[]{:S(2)}) copy-start(bf16[2,2,32]{2,1,0:T(2,128)(2,1)} %param.20) | copy-start | bytes 772
  16.3 49.5 %copy-start.61 = (f32[14,14]{1,0:T(8,128)}, f32[14,14]{1,0:T(8,128)S(1)}, u32[]{:S(2)}) copy-start(f32[14,14]{1,0:T(8,128)S(1)} %broadcast_multiply_fusion.3) | copy-start | bytes 2356
  17.3 50.3 %copy-start.71 = (f32[14,14]{1,0:T(8,128)}, f32[14,14]{1,0:T(8,128)S(1)}, u32[]{:S(2)}) copy-start(f32[14,14]{1,0:T(8,128)S(1)} %multiply_reduce_fusion.13) | copy-start | bytes 2356
  17.3 50.3 %copy-start.69 = (f32[14,14]{1,0:T(8,128)}, f32[14,14]{1,0:T(8,128)S(1)}, u32[]{:S(2)}) copy-start(f32[14,14]{1,0:T(8,128)S(1)} %fusion.110) | copy-start | bytes 2356
  44.5 23.3 %copy-start.79 = (f32[512]{0:T(512)}, f32[512]{0:T(512)S(1)}, u32[]{:S(2)}) copy-start(f32[512]{0:T(512)S(1)} %get-tuple-element.102) | copy-start | bytes 6148
  44.5 238.0 %copy-start.81 = (f32[512]{0:T(512)}, f32[512]{0:T(512)S(1)}, u32[]{:S(2)}) copy-start(f32[512]{0:T(512)S(1)} %get-tuple-element.101) | copy-start | bytes 6148
  44.5 23.3 %copy-start.109 = (bf16[2,4,32]{2,1,0:T(4,128)(2,1)S(1)}, bf16[2,4,32]{2,1,0:T(4,128)(2,1)}, u32[]{:S(2)}) copy-start(bf16[2,4,32]{2,1,0:T(4,128)(2,1)} %param.21) | copy-start | bytes 1540
  67.8 193.3 %copy-start.39 = (bf16[196,512]{1,0:T(8,128)(2,1)}, bf16[196,512]{1,0:T(8,128)(2,1)S(1)}, u32[]{:S(2)}) copy-start(bf16[196,512]{1,0:T(8,128)(2,1)S(1)} %reshape_reshape.24) | copy-start | bytes 602116
  67.9 28.2 %copy-start.78 = (bf16[2,32,512]{2,1,0:T(8,128)(2,1)S(1)}, bf16[2,32,512]{2,1,0:T(8,128)(2,1)}, u32[]{:S(2)}) copy-start(bf16[2,32,512]{2,1,0:T(8,128)(2,1)} %param.16) | copy-start | bytes 196612
  88.9 26.7 %copy-start.110 = (bf16[2,128]{1,0:T(2,128)(2,1)S(1)}, bf16[2,128]{1,0:T(2,128)(2,1)}, u32[]{:S(2)}) copy-start(bf16[2,128]{1,0:T(2,128)(2,1)} %param.22) | copy-start | bytes 1540
  115.5 162.2 %copy-start.4 = (bf16[1,512,512]{2,1,0:T(8,128)(2,1)}, bf16[1,512,512]{2,1,0:T(8,128)(2,1)S(1)}, u32[]{:S(2)}) copy-start(bf16[1,512,512]{2,1,0:T(8,128)(2,1)S(1)} %all-gather.4) | copy-start | bytes 1572868
  156.0 142.1 %copy-start.83 = (f32[512]{0:T(512)}, f32[512]{0:T(512)S(1)}, u32[]{:S(2)}) copy-start(f32[512]{0:T(512)S(1)} %get-tuple-element.94) | copy-start | bytes 6148
  179.4 40.2 %copy-start.97 = (s32[1,14,14]{2,0,1:T(1,128)S(1)}, s32[1,14,14]{2,0,1:T(1,128)}, u32[]{:S(2)}) copy-start(s32[1,14,14]{2,0,1:T(1,128)} %param.14) | copy-start | bytes 2356
  211.1 49.2 %copy-start.25 = (bf16[1,14,14,512]{3,2,1,0:T(8,128)(2,1)S(1)}, bf16[1,14,14,512]{3,2,1,0:T(8,128)(2,1)}, u32[]{:S(2)}) copy-start(bf16[1,14,14,512]{3,2,1,0:T(8,128)(2,1)} %param.13) | copy-start | bytes 602116
  269.6 5.5 copy-start.37
  283.9 7.4 copy-start.42
  309.0 7.5 copy-start.31
  323.0 5.7 copy-start.21
  354.8 5.4 copy-start.86
  360.3 5.4 copy-start.26
  408.8 4.8 copy-start.28
  410.5 8.9 copy-start.76
  432.3 7.2 copy-start.35
  442.4 8.6 copy-start.29
  442.4 5.1 copy-start.6
  450.9 121.3 %reduce-scatter.31.cloned.1.call-start = ((), (), s32[]{:S(2)}) async-start(), calls=%async_computation.16 | async-start | bytes 557056 | tf_op jit(solution)/shard_map/reduce_scatter | solution.py:304
  454.8 5.4 copy-start.38
  460.2 166.5 %reduce-scatter.27.cloned.1.call-start = ((), (), s32[]{:S(2)}) async-start(), calls=%async_computation.14 | async-start | bytes 1671168 | tf_op jit(solution)/shard_map/reduce_scatter | solution.py:301
  466.2 223.0 %reduce-scatter.29.cloned.1.call-start = ((), (), s32[]{:S(2)}) async-start(), calls=%async_computation.15 | async-start | bytes 1671168 | tf_op jit(solution)/shard_map/reduce_scatter | solution.py:301
  468.1 285.4 %reduce-scatter.37.cloned.1.call-start = ((), (), s32[]{:S(2)}) async-start(), calls=%async_computation.19 | async-start | bytes 2228224 | tf_op jit(solution)/shard_map/reduce_scatter | solution.py:318
  471.4 346.8 %reduce-scatter.35.cloned.1.call-start = ((), (), s32[]{:S(2)}) async-start(), calls=%async_computation.18 | async-start | bytes 2228224 | tf_op jit(solution)/shard_map/reduce_scatter | solution.py:318
  474.6 407.8 %reduce-scatter.39.cloned.1.call-start = ((), (), s32[]{:S(2)}) async-start(), calls=%async_computation.20 | async-start | bytes 2228224 | tf_op jit(solution)/shard_map/reduce_scatter | solution.py:321
  478.0 469.1 %reduce-scatter.41.cloned.1.call-start = ((), (), s32[]{:S(2)}) async-start(), calls=%async_computation.21 | async-start | bytes 2228224 | tf_op jit(solution)/shard_map/reduce_scatter | solution.py:321
  481.4 523.2 %reduce-scatter.47.cloned.1.call-start = ((), (), s32[]{:S(2)}) async-start(), calls=%async_computation.30 | async-start | bytes 139264
  487.7 5.6 copy-start.72
  488.2 9.5 copy-start.105
  488.2 9.5 copy-start.107
  488.2 9.5 copy-start.108
  489.1 41.2 %copy-start.103 = (bf16[512]{0:T(512)(128)(2,1)S(1)}, bf16[512]{0:T(512)(128)(2,1)}, u32[]{:S(2)}) copy-start(bf16[512]{0:T(512)(128)(2,1)} %get-tuple-element.79) | copy-start | bytes 3076
  489.1 41.2 %copy-start.98 = (bf16[512]{0:T(512)(128)(2,1)S(1)}, bf16[512]{0:T(512)(128)(2,1)}, u32[]{:S(2)}) copy-start(bf16[512]{0:T(512)(128)(2,1)} %get-tuple-element.81) | copy-start | bytes 3076
  489.1 41.6 %copy-start.104 = (bf16[512]{0:T(512)(128)(2,1)S(1)}, bf16[512]{0:T(512)(128)(2,1)}, u32[]{:S(2)}) copy-start(bf16[512]{0:T(512)(128)(2,1)} %get-tuple-element.85) | copy-start | bytes 3076
  489.1 41.6 %copy-start.102 = (bf16[512]{0:T(512)(128)(2,1)S(1)}, bf16[512]{0:T(512)(128)(2,1)}, u32[]{:S(2)}) copy-start(bf16[512]{0:T(512)(128)(2,1)} %get-tuple-element.87) | copy-start | bytes 3076
  489.2 41.6 %copy-start.99 = (bf16[512]{0:T(512)(128)(2,1)S(1)}, bf16[512]{0:T(512)(128)(2,1)}, u32[]{:S(2)}) copy-start(bf16[512]{0:T(512)(128)(2,1)} %get-tuple-element.119) | copy-start | bytes 3076
  489.2 41.6 %copy-start.100 = (bf16[512]{0:T(512)(128)(2,1)S(1)}, bf16[512]{0:T(512)(128)(2,1)}, u32[]{:S(2)}) copy-start(bf16[512]{0:T(512)(128)(2,1)} %get-tuple-element.145) | copy-start | bytes 3076
  489.2 41.6 %copy-start.87 = (bf16[16,32]{1,0:T(8,128)(2,1)S(1)}, bf16[16,32]{1,0:T(8,128)(2,1)}, u32[]{:S(2)}) copy-start(bf16[16,32]{1,0:T(8,128)(2,1)} %get-tuple-element.182) | copy-start | bytes 3076
  489.2 42.7 %copy-start.96 = (bf16[1,512]{1,0:T(2,128)(2,1)S(1)}, bf16[1,512]{1,0:T(2,128)(2,1)}, u32[]{:S(2)}) copy-start(bf16[1,512]{1,0:T(2,128)(2,1)} %stack.220) | copy-start | bytes 3076
  490.1 43.4 %copy-start.33 = (bf16[1,14,14,512]{3,0,2,1:T(2,128)(2,1)S(1)}, bf16[1,14,14,512]{3,0,2,1:T(2,128)(2,1)}, u32[]{:S(2)}) copy-start(bf16[1,14,14,512]{3,0,2,1:T(2,128)(2,1)} %get-tuple-element.147) | copy-start | bytes 602116
  496.8 565.2 %reduce-scatter.49.cloned.1.call-start = ((), (), s32[]{:S(2)}) async-start(), calls=%async_computation.31 | async-start | bytes 139264
  529.4 590.0 %reduce-scatter.43.cloned.1.call-start = ((), (), s32[]{:S(2)}) async-start(), calls=%async_computation.28 | async-start | bytes 139264
  530.4 647.1 %reduce-scatter.45.cloned.1.call-start = ((), (), s32[]{:S(2)}) async-start(), calls=%async_computation.29 | async-start | bytes 139264
  531.8 703.2 %reduce-scatter.51.cloned.1.call-start = ((), (), s32[]{:S(2)}) async-start(), calls=%async_computation.32 | async-start | bytes 139264
  533.6 415.3 %copy-start.34 = (f32[1,14,14,512]{3,0,2,1:T(1,128)S(1)}, f32[1,14,14,512]{3,0,2,1:T(1,128)}, u32[]{:S(2)}) copy-start(f32[1,14,14,512]{3,0,2,1:T(1,128)} %get-tuple-element.127) | copy-start | bytes 1204228
  534.3 758.2 %reduce-scatter.53.cloned.1.call-start = ((), (), s32[]{:S(2)}) async-start(), calls=%async_computation.33 | async-start | bytes 139264
  572.1 757.3 %all-reduce.7.cloned.1.call-start = ((), (), s32[]{:S(2)}) async-start(), calls=%async_computation.34 | async-start | bytes 1572864 | tf_op jit(solution)/shard_map/psum | solution.py:71
  (73 other events, 160.0 us)
Sparse Core Ops, SparseCore 0:
  10.9 42.7 all-gather.22
  56.4 40.3 all-gather.24
  99.5 40.4 all-gather.26
  142.1 38.9 all-gather.28
  183.7 40.5 all-gather.30
  226.9 40.4 all-gather.32
  451.1 53.9 reduce-scatter.32
  509.6 54.7 reduce-scatter.30
  568.1 58.5 reduce-scatter.26
  630.6 58.4 reduce-scatter.28
  692.9 60.5 reduce-scatter.36
  757.6 60.5 reduce-scatter.34
  821.9 60.4 reduce-scatter.38
  886.5 60.5 reduce-scatter.40
  950.4 54.0 reduce-scatter.46
  1007.8 54.1 reduce-scatter.48
  1065.3 54.0 reduce-scatter.42
  1123.3 54.0 reduce-scatter.44
  1180.9 54.0 reduce-scatter.50
  1238.3 54.0 reduce-scatter.52
  1295.5 33.8 all-reduce.6
where the time goes:
time: 1350 us; the launch traced here: 1340 us
  waiting for transfers between devices  739 us (55%)
  blocking collectives  284 us (21%)
  local copies, waits for them, and re-layouts  132 us (10%)
  other arithmetic  84.2 us (6%)
  matrix products  84.1 us (6%)
  between operations  17.4 us (1%)
    unnamed x27, waiting for transfers between devices  340 us
    reduce_scatter x2, waiting for transfers between devices, body(): lax.psum_scatter(grad_w_first.astype(jnp.bfloat16), 'shard', scatter_dime...  127 us
    reduce_scatter x2, waiting for transfers between devices, body(): lax.psum_scatter(grad_w_second.astype(jnp.bfloat16), 'shard', scatter_dim...  127 us
    reduce_scatter x2, waiting for transfers between devices, body(): lax.psum_scatter(grad_w_proj_qkv.astype(jnp.bfloat16), 'shard', scatter_d...  116 us
    all_gather x2, blocking collectives, body(): lax.all_gather(branch_biases[layer_num], 'shard', axis=1, tiled=True)  52.1 us
    all_gather x2, blocking collectives, body(): lax.all_gather(norm_gains[layer_num], 'shard', axis=1, tiled=True)  42.1 us
    all_gather x2, blocking collectives, body(): lax.all_gather(w_proj[layer_num], 'shard', axis=0, tiled=True)  41.2 us
    all_gather x2, blocking collectives, body(): lax.all_gather(norm_shifts[layer_num], 'shard', axis=1, tiled=True)  37.8 us
  transfers between devices with their start and end apart: 21, of which 13 were waited for; matrix products, arithmetic and copies ran while one was open for 13% of the time, Pallas kernels for 0%

commit v1 on v0

--- a/solution.py
+++ b/solution.py
@@ -337,7 +337,7 @@
         )
     stacked = [jnp.stack([layer_grads[n][m] for n in range(layer_count)]) for m in range(8)]
     summed = replica_total(stacked)
-    table_total = lax.psum(jnp.stack(table_list), ("rep", "shard"))
+    table_total = lax.psum(lax.psum(jnp.stack(table_list), "shard"), "rep")
     return (
         images_out,
         upstream,

time: 1350 us -> 1350 us (level)
  blocking collectives: 284 us -> 313 us
  waiting for transfers between devices: 739 us -> 710 us
    reduce_scatter x2, waiting for transfers between devices: 116 us -> 86.4 us  [body(): lax.psum_scatter(grad_w_proj_qkv.astype(jnp.bfloat16), 'shard', scatter_d...]
    psum x1 -> x2, blocking collectives: 37.7 us -> 66.7 us  [body(): table_total = lax.psum(lax.psum(jnp.stack(table_list), 'shard'), 'rep')]
where the time goes in v1:
time: 1350 us; the launch traced here: 1340 us
  waiting for transfers between devices  710 us (53%)
  blocking collectives  313 us (23%)
  local copies, waits for them, and re-layouts  131 us (10%)
  matrix products  85.1 us (6%)
  other arithmetic  84.2 us (6%)
  between operations  17.4 us (1%)
    unnamed x27, waiting for transfers between devices  340 us
    reduce_scatter x2, waiting for transfers between devices, body(): lax.psum_scatter(grad_w_second.astype(jnp.bfloat16), 'shard', scatter_dim...  127 us
    reduce_scatter x2, waiting for transfers between devices, body(): lax.psum_scatter(grad_w_first.astype(jnp.bfloat16), 'shard', scatter_dime...  127 us
    reduce_scatter x2, waiting for transfers between devices, body(): lax.psum_scatter(grad_w_proj_qkv.astype(jnp.bfloat16), 'shard', scatter_d...  86.4 us
    psum x2, blocking collectives, body(): table_total = lax.psum(lax.psum(jnp.stack(table_list), 'shard'), 'rep')  66.7 us
    all_gather x2, blocking collectives, body(): lax.all_gather(branch_biases[layer_num], 'shard', axis=1, tiled=True)  51.7 us
    all_gather x2, blocking collectives, body(): lax.all_gather(norm_gains[layer_num], 'shard', axis=1, tiled=True)  42.7 us
    all_gather x2, blocking collectives, body(): lax.all_gather(w_proj[layer_num], 'shard', axis=0, tiled=True)  41.1 us
  transfers between devices with their start and end apart: 21, of which 13 were waited for; matrix products, arithmetic and copies ran while one was open for 13% of the time, Pallas kernels for 0%

profile of v1, /device:TPU:0, one launch (start us, length us, event | category | flops | bytes accessed | tf_op | source)
XLA Modules:
  0.0 1342.0 jit_solution(1424240670160909906)
XLA Ops:
  17.5 24.1 %all-gather = bf16[1,2,512]{1,0,2:T(2,128)(2,1)S(1)} all-gather(bf16[1,2,32]{1,0,2:T(2,128)(2,1)S(1)} %copy.412), channel_id=2, replica_groups=mesh['rep'=2,'shard'=16] {'shard'}, dimensions={2}, use_global_device_ids=true | all-gather | bytes 2176 | tf_op jit(solution)/shard_map/all_gather | solution.py:134
  41.9 2.7 slice_reduce_fusion.10
  44.8 18.6 %all-gather.1 = bf16[1,2,512]{1,0,2:T(2,128)(2,1)S(1)} all-gather(bf16[1,2,32]{1,0,2:T(2,128)(2,1)S(1)} %copy.413), channel_id=3, replica_groups=mesh['rep'=2,'shard'=16] {'shard'}, dimensions={2}, use_global_device_ids=true | all-gather | bytes 2176 | tf_op jit(solution)/shard_map/all_gather | solution.py:135
  63.6 2.7 slice_reduce_fusion.9
  68.4 20.2 %all-gather.3 = bf16[1,4,512]{1,0,2:T(2,128)(2,1)S(1)} all-gather(bf16[1,4,32]{1,0,2:T(2,128)(2,1)S(1)} %copy.414), channel_id=5, replica_groups=mesh['rep'=2,'shard'=16] {'shard'}, dimensions={2}, use_global_device_ids=true | all-gather | bytes 4352 | tf_op jit(solution)/shard_map/all_gather | solution.py:136
  88.9 6.7 slice_reduce_fusion.8
  96.1 19.5 %all-gather.4 = bf16[1,512,512]{2,1,0:T(8,128)(2,1)S(1)} all-gather(bf16[1,32,512]{2,1,0:T(8,128)(2,1)S(1)} %get-tuple-element.155), channel_id=6, replica_groups=mesh['rep'=2,'shard'=16] {'shard'}, dimensions={1}, use_global_device_ids=true | all-gather | bytes 557056 | tf_op jit(solution)/shard_map/all_gather | solution.py:133
  115.6 18.2 %all-gather.6 = bf16[1,2048]{1,0:T(2,128)(2,1)S(1)} all-gather(bf16[1,128]{1,0:T(2,128)(2,1)S(1)} %get-tuple-element.163), channel_id=8, replica_groups=mesh['rep'=2,'shard'=16] {'shard'}, dimensions={1}, use_global_device_ids=true | all-gather | bytes 4352 | tf_op jit(solution)/shard_map/all_gather | solution.py:141
  133.9 18.6 %all-gather.8 = bf16[1,2,512]{1,0,2:T(2,128)(2,1)S(1)} all-gather(bf16[1,2,32]{1,0,2:T(2,128)(2,1)S(1)} %copy.415), channel_id=10, replica_groups=mesh['rep'=2,'shard'=16] {'shard'}, dimensions={2}, use_global_device_ids=true | all-gather | bytes 2176 | tf_op jit(solution)/shard_map/all_gather | solution.py:134
  152.8 3.3 slice_reduce_fusion.2
  156.2 19.2 %all-gather.9 = bf16[1,2,512]{1,0,2:T(2,128)(2,1)S(1)} all-gather(bf16[1,2,32]{1,0,2:T(2,128)(2,1)S(1)} %copy.416), channel_id=11, replica_groups=mesh['rep'=2,'shard'=16] {'shard'}, dimensions={2}, use_global_device_ids=true | all-gather | bytes 2176 | tf_op jit(solution)/shard_map/all_gather | solution.py:135
  175.7 3.3 slice_reduce_fusion.1
  179.2 31.5 %all-gather.11 = bf16[1,4,512]{1,0,2:T(2,128)(2,1)S(1)} all-gather(bf16[1,4,32]{1,0,2:T(2,128)(2,1)S(1)} %copy.417), channel_id=13, replica_groups=mesh['rep'=2,'shard'=16] {'shard'}, dimensions={2}, use_global_device_ids=true | all-gather | bytes 4352 | tf_op jit(solution)/shard_map/all_gather | solution.py:136
  211.0 7.3 slice_reduce_fusion
  220.4 21.6 %all-gather.12 = bf16[1,512,512]{2,1,0:T(8,128)(2,1)} all-gather(bf16[1,32,512]{2,1,0:T(8,128)(2,1)S(1)} %get-tuple-element.154), channel_id=14, replica_groups=mesh['rep'=2,'shard'=16] {'shard'}, dimensions={1}, use_global_device_ids=true | all-gather | bytes 557056 | tf_op jit(solution)/shard_map/all_gather | solution.py:133
  242.0 17.6 %all-gather.14 = bf16[1,2048]{1,0:T(2,128)(2,1)S(1)} all-gather(bf16[1,128]{1,0:T(2,128)(2,1)S(1)} %get-tuple-element.162), channel_id=16, replica_groups=mesh['rep'=2,'shard'=16] {'shard'}, dimensions={1}, use_global_device_ids=true | all-gather | bytes 4352 | tf_op jit(solution)/shard_map/all_gather | solution.py:141
  270.8 2.6 copy.312
  283.8 7.4 fusion.20
  291.1 3.2 fusion.57
  304.9 2.6 copy.324
  308.8 2.6 copy.325
  311.5 2.3 reshape.792
  313.7 2.6 copy.328
  334.1 7.0 fusion.23
  341.1 3.9 fusion.150
  349.5 4.6 multiply_reduce_fusion.2
  354.7 3.2 fusion.60
  357.8 2.3 reshape.774
  360.1 5.4 fusion.130
  377.4 2.3 reshape.796
  379.7 2.6 copy.337
  382.3 2.7 multiply_reduce_fusion.1
  394.0 2.2 copy.347
  398.3 2.2 copy.341
  404.1 2.7 convolution_add_fusion.3
  414.5 4.8 multiply_reduce_fusion.3
  419.3 4.3 fusion.129
  423.6 2.7 convert_reduce_fusion.6
  426.4 3.9 fusion.151
  432.2 3.7 multiply_reduce_fusion.4
  435.9 3.4 fusion.128
  439.3 2.7 convert_reduce_fusion.4
  443.2 2.3 reshape.798
  447.4 3.4 multiply_reduce_fusion
  451.1 3.0 convert_reduce_fusion.1
  488.4 31.7 %all-reduce.2 = (bf16[2048]{0:T(1024)(128)(2,1)S(1)}, bf16[2048]{0:T(1024)(128)(2,1)S(1)}) all-reduce(bf16[2048]{0:T(1024)(128)(2,1)S(1)} %copy-done.105, bf16[2048]{0:T(1024)(128)(2,1)S(1)} %copy-done.106), channel_id=33, replica_groups=mesh['rep'=2,'shard'=16] {'shard'}, use_global_device_ids=true, to_apply=%region_63.64.clone | all-reduce | flops 4096 | bytes 16384
  522.2 3.1 multiply_reduce_fusion.5
  525.3 3.4 fusion.127
  532.0 57.7 %psum.78 = f32[2,169,16]{1,2,0:T(8,128)S(1)} all-reduce(f32[2,169,16]{1,2,0:T(8,128)S(1)} %pad_maximum_fusion.10), channel_id=1, replica_groups=mesh['rep'=2,'shard'=16] {'shard'}, use_global_device_ids=true, to_apply=%region_67.68 | all-reduce | flops 5408 | bytes 43264 | tf_op jit(solution)/shard_map/psum | solution.py:340
  590.8 9.0 psum.79
  602.9 23.8 %reduce-scatter.27.cloned.1.call-done = bf16[32,1536]{1,0:T(8,128)(2,1)} async-done(((bf16[512,1536]{1,0:T(8,128)(2,1)}), bf16[32,1536]{1,0:T(8,128)(2,1)}) %reduce-scatter.27.cloned.1.call-update) | async-done | bytes 98320 | tf_op jit(solution)/shard_map/reduce_scatter | solution.py:301
  626.7 62.5 %reduce-scatter.29.cloned.1.call-done = bf16[32,1536]{1,0:T(8,128)(2,1)} async-done(((bf16[512,1536]{1,0:T(8,128)(2,1)}), bf16[32,1536]{1,0:T(8,128)(2,1)}) %reduce-scatter.29.cloned.1.call-update) | async-done | bytes 98320 | tf_op jit(solution)/shard_map/reduce_scatter | solution.py:301
  690.9 62.7 %reduce-scatter.37.cloned.1.call-done = bf16[32,2048]{1,0:T(8,128)(2,1)} async-done(((bf16[512,2048]{1,0:T(8,128)(2,1)}), bf16[32,2048]{1,0:T(8,128)(2,1)}) %reduce-scatter.37.cloned.1.call-update) | async-done | bytes 131088 | tf_op jit(solution)/shard_map/reduce_scatter | solution.py:318
  753.6 64.6 %reduce-scatter.35.cloned.1.call-done = bf16[32,2048]{1,0:T(8,128)(2,1)} async-done(((bf16[512,2048]{1,0:T(8,128)(2,1)}), bf16[32,2048]{1,0:T(8,128)(2,1)}) %reduce-scatter.35.cloned.1.call-update) | async-done | bytes 131088 | tf_op jit(solution)/shard_map/reduce_scatter | solution.py:318
  819.9 62.7 %reduce-scatter.39.cloned.1.call-done = bf16[128,512]{1,0:T(8,128)(2,1)} async-done(((bf16[2048,512]{1,0:T(8,128)(2,1)}), bf16[128,512]{1,0:T(8,128)(2,1)}) %reduce-scatter.39.cloned.1.call-update) | async-done | bytes 131088 | tf_op jit(solution)/shard_map/reduce_scatter | solution.py:321
  882.6 64.7 %reduce-scatter.41.cloned.1.call-done = bf16[128,512]{1,0:T(8,128)(2,1)} async-done(((bf16[2048,512]{1,0:T(8,128)(2,1)}), bf16[128,512]{1,0:T(8,128)(2,1)}) %reduce-scatter.41.cloned.1.call-update) | async-done | bytes 131088 | tf_op jit(solution)/shard_map/reduce_scatter | solution.py:321
  950.2 54.4 %reduce-scatter.47.cloned.1.call-done = bf16[32,2]{1,0:T(8,128)(2,1)} async-done(((bf16[512,2]{1,0:T(8,128)(2,1)}), bf16[32,2]{1,0:T(8,128)(2,1)}) %reduce-scatter.47.cloned.1.call-update) | async-done | bytes 144
  1005.4 56.7 %reduce-scatter.49.cloned.1.call-done = bf16[32,2]{1,0:T(8,128)(2,1)} async-done(((bf16[512,2]{1,0:T(8,128)(2,1)}), bf16[32,2]{1,0:T(8,128)(2,1)}) %reduce-scatter.49.cloned.1.call-update) | async-done | bytes 144
  1062.9 56.7 %reduce-scatter.43.cloned.1.call-done = bf16[32,2]{1,0:T(8,128)(2,1)} async-done(((bf16[512,2]{1,0:T(8,128)(2,1)}), bf16[32,2]{1,0:T(8,128)(2,1)}) %reduce-scatter.43.cloned.1.call-update) | async-done | bytes 144
  1120.3 57.3 %reduce-scatter.45.cloned.1.call-done = bf16[32,2]{1,0:T(8,128)(2,1)} async-done(((bf16[512,2]{1,0:T(8,128)(2,1)}), bf16[32,2]{1,0:T(8,128)(2,1)}) %reduce-scatter.45.cloned.1.call-update) | async-done | bytes 144
  1178.4 56.8 %reduce-scatter.51.cloned.1.call-done = bf16[32,4]{1,0:T(8,128)(2,1)} async-done(((bf16[512,4]{1,0:T(8,128)(2,1)}), bf16[32,4]{1,0:T(8,128)(2,1)}) %reduce-scatter.51.cloned.1.call-update) | async-done | bytes 272
  1235.9 56.7 %reduce-scatter.53.cloned.1.call-done = bf16[32,4]{1,0:T(8,128)(2,1)} async-done(((bf16[512,4]{1,0:T(8,128)(2,1)}), bf16[32,4]{1,0:T(8,128)(2,1)}) %reduce-scatter.53.cloned.1.call-update) | async-done | bytes 272
  1293.4 5.0 all-reduce.3
  1300.7 28.9 %all-reduce.7.cloned.1.call-done = (bf16[2,32,1536]{2,1,0:T(8,128)(2,1)}, bf16[2,32,512]{2,1,0:T(8,128)(2,1)}, bf16[2,32,2048]{2,1,0:T(8,128)(2,1)}, bf16[2,128,512]{2,1,0:T(8,128)(2,1)}) async-done(((bf16[2,32,1536]{2,1,0:T(8,128)(2,1)}, bf16[2,32,512]{2,1,0:T(8,128)(2,1)}, bf16[2,32,2048]{2,1,0:T(8,128)(2,1)}, bf16[2,128,512]{2,1,0:T(8,128)(2,1)}), (bf16[2,32,1536]{2,1,0:T(8,128)(2,1)}, ...) | async-done | bytes 786448 | tf_op jit(solution)/shard_map/psum | solution.py:71
  (513 shorter events, 172.4 us)
Async XLA Ops:
  7.2 7.3 copy-start.111
  7.2 253.7 %all-gather.23.cloned.1.call-start = ((), (), s32[]{:S(2)}) async-start(), calls=%async_computation.22 | async-start | bytes 1671168 | tf_op jit(solution)/shard_map/all_gather | solution.py:132
  8.9 6.8 copy-start.2
  8.9 274.9 %all-gather.25.cloned.1.call-start = ((), (), s32[]{:S(2)}) async-start(), calls=%async_computation.23 | async-start | bytes 2228224 | tf_op jit(solution)/shard_map/all_gather | solution.py:139
  10.7 6.7 copy-start.109
  10.7 280.4 %all-gather.27.cloned.1.call-start = ((), (), s32[]{:S(2)}) async-start(), calls=%async_computation.24 | async-start | bytes 2228224 | tf_op jit(solution)/shard_map/all_gather | solution.py:140
  12.4 288.3 %all-gather.29.cloned.1.call-start = ((), (), s32[]{:S(2)}) async-start(), calls=%async_computation.25 | async-start | bytes 1671168 | tf_op jit(solution)/shard_map/all_gather | solution.py:132
  13.0 321.1 %all-gather.31.cloned.1.call-start = ((), (), s32[]{:S(2)}) async-start(), calls=%async_computation.26 | async-start | bytes 2228224 | tf_op jit(solution)/shard_map/all_gather | solution.py:139
  13.6 327.5 %all-gather.33.cloned.1.call-start = ((), (), s32[]{:S(2)}) async-start(), calls=%async_computation.27 | async-start | bytes 2228224 | tf_op jit(solution)/shard_map/all_gather | solution.py:140
  14.2 587.3 %reduce-scatter.33.cloned.1.call-start = ((), (), s32[]{:S(2)}) async-start(), calls=%async_computation.17 | async-start | bytes 557056 | tf_op jit(solution)/shard_map/reduce_scatter | solution.py:304
  14.3 30.3 %copy-start.110 = (bf16[2,2,32]{2,1,0:T(2,128)(2,1)S(1)}, bf16[2,2,32]{2,1,0:T(2,128)(2,1)}, u32[]{:S(2)}) copy-start(bf16[2,2,32]{2,1,0:T(2,128)(2,1)} %param.20) | copy-start | bytes 772
  16.3 50.0 %copy-start.60 = (f32[14,14]{1,0:T(8,128)}, f32[14,14]{1,0:T(8,128)S(1)}, u32[]{:S(2)}) copy-start(f32[14,14]{1,0:T(8,128)S(1)} %broadcast_multiply_fusion.3) | copy-start | bytes 2356
  17.3 50.8 %copy-start.70 = (f32[14,14]{1,0:T(8,128)}, f32[14,14]{1,0:T(8,128)S(1)}, u32[]{:S(2)}) copy-start(f32[14,14]{1,0:T(8,128)S(1)} %multiply_reduce_fusion.13) | copy-start | bytes 2356
  17.4 49.0 %copy-start.68 = (f32[14,14]{1,0:T(8,128)}, f32[14,14]{1,0:T(8,128)S(1)}, u32[]{:S(2)}) copy-start(f32[14,14]{1,0:T(8,128)S(1)} %fusion.110) | copy-start | bytes 2356
  44.6 21.7 %copy-start.78 = (f32[512]{0:T(512)}, f32[512]{0:T(512)S(1)}, u32[]{:S(2)}) copy-start(f32[512]{0:T(512)S(1)} %get-tuple-element.102) | copy-start | bytes 6148
  44.6 237.6 %copy-start.80 = (f32[512]{0:T(512)}, f32[512]{0:T(512)S(1)}, u32[]{:S(2)}) copy-start(f32[512]{0:T(512)S(1)} %get-tuple-element.101) | copy-start | bytes 6148
  44.7 23.6 %copy-start.107 = (bf16[2,4,32]{2,1,0:T(4,128)(2,1)S(1)}, bf16[2,4,32]{2,1,0:T(4,128)(2,1)}, u32[]{:S(2)}) copy-start(bf16[2,4,32]{2,1,0:T(4,128)(2,1)} %param.21) | copy-start | bytes 1540
  68.2 192.7 %copy-start.39 = (bf16[196,512]{1,0:T(8,128)(2,1)}, bf16[196,512]{1,0:T(8,128)(2,1)S(1)}, u32[]{:S(2)}) copy-start(bf16[196,512]{1,0:T(8,128)(2,1)S(1)} %reshape_reshape.24) | copy-start | bytes 602116
  68.4 27.7 %copy-start.77 = (bf16[2,32,512]{2,1,0:T(8,128)(2,1)S(1)}, bf16[2,32,512]{2,1,0:T(8,128)(2,1)}, u32[]{:S(2)}) copy-start(bf16[2,32,512]{2,1,0:T(8,128)(2,1)} %param.16) | copy-start | bytes 196612
  88.9 26.7 %copy-start.108 = (bf16[2,128]{1,0:T(2,128)(2,1)S(1)}, bf16[2,128]{1,0:T(2,128)(2,1)}, u32[]{:S(2)}) copy-start(bf16[2,128]{1,0:T(2,128)(2,1)} %param.22) | copy-start | bytes 1540
  115.6 161.9 %copy-start.4 = (bf16[1,512,512]{2,1,0:T(8,128)(2,1)}, bf16[1,512,512]{2,1,0:T(8,128)(2,1)S(1)}, u32[]{:S(2)}) copy-start(bf16[1,512,512]{2,1,0:T(8,128)(2,1)S(1)} %all-gather.4) | copy-start | bytes 1572868
  156.1 141.9 %copy-start.82 = (f32[512]{0:T(512)}, f32[512]{0:T(512)S(1)}, u32[]{:S(2)}) copy-start(f32[512]{0:T(512)S(1)} %get-tuple-element.94) | copy-start | bytes 6148
  179.2 40.3 %copy-start.95 = (s32[1,14,14]{2,0,1:T(1,128)S(1)}, s32[1,14,14]{2,0,1:T(1,128)}, u32[]{:S(2)}) copy-start(s32[1,14,14]{2,0,1:T(1,128)} %param.14) | copy-start | bytes 2356
  210.9 49.2 %copy-start.25 = (bf16[1,14,14,512]{3,2,1,0:T(8,128)(2,1)S(1)}, bf16[1,14,14,512]{3,2,1,0:T(8,128)(2,1)}, u32[]{:S(2)}) copy-start(bf16[1,14,14,512]{3,2,1,0:T(8,128)(2,1)} %param.13) | copy-start | bytes 602116
  269.4 5.5 copy-start.37
  283.7 7.4 copy-start.42
  308.8 7.5 copy-start.31
  322.9 5.7 copy-start.21
  354.7 5.4 copy-start.85
  410.4 8.9 copy-start.75
  432.2 7.2 copy-start.35
  442.2 8.6 copy-start.29
  450.8 150.7 %reduce-scatter.31.cloned.1.call-start = ((), (), s32[]{:S(2)}) async-start(), calls=%async_computation.16 | async-start | bytes 557056 | tf_op jit(solution)/shard_map/reduce_scatter | solution.py:304
  454.7 5.4 copy-start.38
  460.0 166.7 %reduce-scatter.27.cloned.1.call-start = ((), (), s32[]{:S(2)}) async-start(), calls=%async_computation.14 | async-start | bytes 1671168 | tf_op jit(solution)/shard_map/reduce_scatter | solution.py:301
  466.1 223.2 %reduce-scatter.29.cloned.1.call-start = ((), (), s32[]{:S(2)}) async-start(), calls=%async_computation.15 | async-start | bytes 1671168 | tf_op jit(solution)/shard_map/reduce_scatter | solution.py:301
  468.0 285.6 %reduce-scatter.37.cloned.1.call-start = ((), (), s32[]{:S(2)}) async-start(), calls=%async_computation.19 | async-start | bytes 2228224 | tf_op jit(solution)/shard_map/reduce_scatter | solution.py:318
  471.2 346.9 %reduce-scatter.35.cloned.1.call-start = ((), (), s32[]{:S(2)}) async-start(), calls=%async_computation.18 | async-start | bytes 2228224 | tf_op jit(solution)/shard_map/reduce_scatter | solution.py:318
  474.5 408.1 %reduce-scatter.39.cloned.1.call-start = ((), (), s32[]{:S(2)}) async-start(), calls=%async_computation.20 | async-start | bytes 2228224 | tf_op jit(solution)/shard_map/reduce_scatter | solution.py:321
  477.8 469.4 %reduce-scatter.41.cloned.1.call-start = ((), (), s32[]{:S(2)}) async-start(), calls=%async_computation.21 | async-start | bytes 2228224 | tf_op jit(solution)/shard_map/reduce_scatter | solution.py:321
  481.2 523.4 %reduce-scatter.47.cloned.1.call-start = ((), (), s32[]{:S(2)}) async-start(), calls=%async_computation.30 | async-start | bytes 139264
  486.9 33.2 %copy-start.88 = (s32[2401]{0:T(1024)S(1)}, s32[2401]{0:T(1024)}, u32[]{:S(2)}) copy-start(s32[2401]{0:T(1024)} %copy-done.87) | copy-start | bytes 28816
  487.0 34.2 %copy-start.63 = (f32[16,2401]{1,0:T(8,128)S(1)}, f32[16,2401]{1,0:T(8,128)}, u32[]{:S(2)}) copy-start(f32[16,2401]{1,0:T(8,128)} %reshape.716) | copy-start | bytes 460996
  487.9 34.3 %copy-start.3 = (bf16[1,14,14,512]{3,2,1,0:T(8,128)(2,1)S(1)}, bf16[1,14,14,512]{3,2,1,0:T(8,128)(2,1)}, u32[]{:S(2)}) copy-start(bf16[1,14,14,512]{3,2,1,0:T(8,128)(2,1)} %param.12) | copy-start | bytes 602116
  487.9 34.3 %copy-start.61 = (f32[14,14]{1,0:T(8,128)S(1)}, f32[14,14]{1,0:T(8,128)}, u32[]{:S(2)}) copy-start(f32[14,14]{1,0:T(8,128)} %copy-done.60) | copy-start | bytes 2356
  487.9 34.3 %copy-start.69 = (f32[14,14]{1,0:T(8,128)S(1)}, f32[14,14]{1,0:T(8,128)}, u32[]{:S(2)}) copy-start(f32[14,14]{1,0:T(8,128)} %copy-done.68) | copy-start | bytes 2356
  487.9 34.3 %copy-start.79 = (f32[512]{0:T(512)S(1)}, f32[512]{0:T(512)}, u32[]{:S(2)}) copy-start(f32[512]{0:T(512)} %copy-done.78) | copy-start | bytes 6148
  488.0 37.3 %copy-start.71 = (f32[14,14]{1,0:T(8,128)S(1)}, f32[14,14]{1,0:T(8,128)}, u32[]{:S(2)}) copy-start(f32[14,14]{1,0:T(8,128)} %copy-done.70) | copy-start | bytes 2356
  520.2 9.6 copy-start.103
  521.1 9.6 copy-start.101
  521.1 9.6 copy-start.98
  521.1 9.9 copy-start.102
  521.1 9.9 copy-start.100
  522.1 68.4 %copy-start.96 = (bf16[512]{0:T(512)(128)(2,1)S(1)}, bf16[512]{0:T(512)(128)(2,1)}, u32[]{:S(2)}) copy-start(bf16[512]{0:T(512)(128)(2,1)} %get-tuple-element.119) | copy-start | bytes 3076
  522.1 68.4 %copy-start.97 = (bf16[512]{0:T(512)(128)(2,1)S(1)}, bf16[512]{0:T(512)(128)(2,1)}, u32[]{:S(2)}) copy-start(bf16[512]{0:T(512)(128)(2,1)} %get-tuple-element.145) | copy-start | bytes 3076
  522.1 68.4 %copy-start.86 = (bf16[16,32]{1,0:T(8,128)(2,1)S(1)}, bf16[16,32]{1,0:T(8,128)(2,1)}, u32[]{:S(2)}) copy-start(bf16[16,32]{1,0:T(8,128)(2,1)} %get-tuple-element.182) | copy-start | bytes 3076
  522.2 78.5 %copy-start.33 = (bf16[1,14,14,512]{3,0,2,1:T(2,128)(2,1)S(1)}, bf16[1,14,14,512]{3,0,2,1:T(2,128)(2,1)}, u32[]{:S(2)}) copy-start(bf16[1,14,14,512]{3,0,2,1:T(2,128)(2,1)} %get-tuple-element.147) | copy-start | bytes 602116
  528.8 533.3 %reduce-scatter.49.cloned.1.call-start = ((), (), s32[]{:S(2)}) async-start(), calls=%async_computation.31 | async-start | bytes 139264
  529.8 589.8 %reduce-scatter.43.cloned.1.call-start = ((), (), s32[]{:S(2)}) async-start(), calls=%async_computation.28 | async-start | bytes 139264
  530.8 646.8 %reduce-scatter.45.cloned.1.call-start = ((), (), s32[]{:S(2)}) async-start(), calls=%async_computation.29 | async-start | bytes 139264
  531.9 703.3 %reduce-scatter.51.cloned.1.call-start = ((), (), s32[]{:S(2)}) async-start(), calls=%async_computation.32 | async-start | bytes 139264
  590.7 701.9 %reduce-scatter.53.cloned.1.call-start = ((), (), s32[]{:S(2)}) async-start(), calls=%async_computation.33 | async-start | bytes 139264
  599.8 349.1 %copy-start.34 = (f32[1,14,14,512]{3,0,2,1:T(1,128)S(1)}, f32[1,14,14,512]{3,0,2,1:T(1,128)}, u32[]{:S(2)}) copy-start(f32[1,14,14,512]{3,0,2,1:T(1,128)} %get-tuple-element.127) | copy-start | bytes 1204228
  601.4 728.2 %all-reduce.7.cloned.1.call-start = ((), (), s32[]{:S(2)}) async-start(), calls=%async_computation.34 | async-start | bytes 1572864 | tf_op jit(solution)/shard_map/psum | solution.py:71
  (71 other events, 166.4 us)
Sparse Core Ops, SparseCore 0:
  10.9 42.6 all-gather.22
  56.3 40.3 all-gather.24
  99.4 40.4 all-gather.26
  142.1 38.7 all-gather.28
  183.4 40.6 all-gather.30
  226.7 40.3 all-gather.32
  450.9 54.1 reduce-scatter.32
  509.6 54.8 reduce-scatter.30
  568.2 58.5 reduce-scatter.26
  630.7 58.5 reduce-scatter.28
  693.0 60.5 reduce-scatter.36
  757.6 60.5 reduce-scatter.34
  821.9 60.5 reduce-scatter.38
  886.6 60.5 reduce-scatter.40
  950.5 54.0 reduce-scatter.46
  1008.0 54.0 reduce-scatter.48
  1065.4 54.0 reduce-scatter.42
  1123.4 54.1 reduce-scatter.44
  1181.0 54.0 reduce-scatter.50
  1238.5 54.1 reduce-scatter.52
  1295.7 33.9 all-reduce.6
